TPU v7x, 32 devices: a whole 2x2x4 slice. The times are simulated.
32 devices in a mesh: gx: 4 (over z), gy: 8 (over y, x, core).
Axes of the slice: x: 2, y: 2, z: 4, core: 2. Of those that a mesh axis runs over, the one named last changes fastest.
Arguments:
- source: float32 [128, 256, 128], P('gx', 'gy'), may hold values from -6 to 6
- inverse_density: float32 [128, 256, 128], P('gx', 'gy'), may hold values from 1 to 7
Outputs:
- correction: float32 [128, 256, 128], P('gx', 'gy')
All inputs are finite; a program needn't handle non-finite values.
Results may differ from a plain program's by a relative error of at most 0.0001.
Values sent between devices are 32-bit elements; how exact they have to be, the bound alone decides.
A program may use at most 128 MiB of HBM per device.

v0:
```python
import functools

import jax
import jax.numpy as jnp
from jax import lax
from jax.experimental import pallas as pl
from jax.experimental.pallas import tpu as pltpu
from jax.sharding import PartitionSpec as P

MESH = pl.DeviceIdType.MESH
OMEGA = 0.8
F32 = jnp.float32

PLANES = (42, 16, 12, 5)
ROWS = (48, 32, 40, 24)
UNROLL = (4, 7, 5, 3)
OWN = 32
NEAR = [(dx, dy) for dx in (1, -1, 0) for dy in (0, 1, -1) if (dx, dy) != (0, 0)]


def far_offsets(peers):
    return (-1, 0, 1, 2) if peers == 4 else (-2, -1, 0, 1, 2)


def lanes(value, shift):
    return pltpu.roll(value, shift % 128, 1)


def rows(value, shift):
    return pltpu.roll(value, shift % value.shape[0], 0)


def lane_index(height):
    return lax.broadcasted_iota(jnp.int32, (height, 128), 1)


def swap_lanes(value, step):
    low = (lane_index(value.shape[0]) & step) == 0
    return jnp.where(low, lanes(value, -step), lanes(value, step))


def loop(first, last, body, unroll=2):
    count = last - first
    whole = count // unroll if count > unroll else 0

    def step(trip, carry):
        for inner in range(unroll):
            body(first + trip * unroll + inner)
        return carry

    if whole:
        lax.fori_loop(0, whole, step, 0)
    for index in range(first + whole * unroll, last):
        body(index)


def bit(number, height):
    return (lane_index(height) & number) != 0


def place_in_group(level, height):
    return lane_index(height) & (2**level - 1)


def next_x(level, here, after):
    if level == 0:
        return after
    size = 2**level
    last = place_in_group(level, here.shape[0]) == size - 1
    return jnp.where(last, lanes(after, size - 1), lanes(here, -1))


def previous_x(level, here, before):
    if level == 0:
        return before
    size = 2**level
    first = place_in_group(level, here.shape[0]) == 0
    return jnp.where(first, lanes(before, 1 - size), lanes(here, 1))


def build(level, first, last, b, cx, cxm, cy, cz, diag, gain, f=None, u=None):
    height = ROWS[level]
    factor2 = 2.0 * 0.25**level
    step = 2**level
    lane = lane_index(height)
    top = lane >= 128 - step
    ends = top | (lane < step)

    def pair(left, right):
        return factor2 * left * right / (left + right)

    def one(x, carry):
        c_before, here = carry
        after = b[x + 1]
        c_x = pair(here, next_x(level, here, after))
        c_m = previous_x(level, c_x, c_before)
        c_y = pair(here, rows(here, -1))
        c_z = jnp.where(top, 0.0, pair(here, lanes(here, -step)))
        total = c_m + c_x + c_y + rows(c_y, 1) + c_z + lanes(c_z, step)
        total = total + jnp.where(ends, (0.5 * factor2) * here, 0.0)
        scaled = OMEGA / total
        cx[x] = c_x
        if level > 0:
            cxm[x] = c_m
        cy[x] = c_y
        cz[x] = c_z
        diag[x] = total
        gain[x] = scaled
        if f is not None:
            u[x] = scaled * f[x]
        return (c_x, after)

    before = pair(b[first - 1], next_x(level, b[first - 1], b[first]))
    cx[first - 1] = before
    count = last - first
    carry = (before, b[first])
    if count < 6:
        for x in range(first, last):
            carry = one(x, carry)
        return

    def two(trip, carry):
        carry = one(first + 2 * trip, carry)
        return one(first + 1 + 2 * trip, carry)

    lax.fori_loop(0, count // 2, two, carry)


def first_sweep(level, first, last, u, f, gain):
    def one(x):
        u[x] = gain[x] * f[x]

    loop(first, last, one, UNROLL[level])


def spread(level, x, u, cx, cxm, cy, cz, span):
    here = u[x, span]
    along_y = cy[x, span]
    along_z = cz[x, span]
    step = 2**level
    lower = cx[x - 1, span] if level == 0 else cxm[x, span]
    total = cx[x, span] * next_x(level, here, u[x + 1, span])
    total = total + lower * previous_x(level, here, u[x - 1, span])
    total = total + (along_y * rows(here, -1) + rows(along_y * here, 1))
    total = total + (along_z * lanes(here, -step) + lanes(along_z * here, step))
    return here, total


def sweep(level, first, last, source, target, f, cx, cxm, cy, cz, gain, span=None):
    span = pl.ds(0, ROWS[level]) if span is None else span

    def one(x):
        here, total = spread(level, x, source, cx, cxm, cy, cz, span)
        target[x, span] = (1.0 - OMEGA) * here + gain[x, span] * (f[x, span] + total)

    loop(first, last, one, UNROLL[level])


def coarsen(level, values):
    height = values[0].shape[0]
    if level == 0:
        even = ~bit(1, height)
        left, right = values[0] + values[1], values[2] + values[3]
        return jnp.where(even, left, right) + jnp.where(even, lanes(left, -1), lanes(right, 1))
    size = 2**level
    sums = []
    for value in values:
        value = value + swap_lanes(value, 1)
        value = value + swap_lanes(value, size)
        if level == 2:
            value = jnp.where(bit(2, height) == bit(1, height), value, swap_lanes(value, 2))
        sums.append(value)
    low, high = (1, 2) if level == 1 else (2, 4)
    lower = jnp.where(bit(low, height), sums[1], sums[0])
    upper = jnp.where(bit(low, height), sums[3], sums[2])
    return jnp.where(bit(high, height), upper, lower)


def refine(level, value):
    height = value.shape[0]
    if level == 0:
        other = swap_lanes(value, 1)
        low = jnp.where(bit(1, height), other, value)
        high = jnp.where(bit(1, height), value, other)
        return [low, low, high, high]
    outer, inner = (2, 1) if level == 1 else (4, 2)
    other = swap_lanes(value, outer)
    result = []
    for half in (jnp.where(bit(outer, height), other, value), jnp.where(bit(outer, height), value, other)):
        swapped = swap_lanes(half, inner)
        result.append(jnp.where(bit(inner, height), swapped, half))
        result.append(jnp.where(bit(inner, height), half, swapped))
    if level == 2:
        same = bit(2, height) == bit(1, height)
        result = [jnp.where(same, part, swap_lanes(part, 1)) for part in result]
    return result


def pair_rows(tmp, slot, value):
    count = value.shape[0] // 2
    tmp[slot, pl.ds(0, 2 * count)] = value
    summed = tmp[slot, pl.ds(0, count, stride=2)] + tmp[slot, pl.ds(1, count, stride=2)]
    return 0.125 * summed


def restrict(level, plane, target, tmp, fine_x, planes, count, at_x, at_row, limit=None):
    def one(i):
        parts = [fine_x + 4 * i + m for m in range(4)]
        if limit is not None:
            parts = [min(part, limit) for part in parts]
        value = coarsen(level, [plane(part) for part in parts])
        target[at_x + i, pl.ds(at_row, count)] = pair_rows(tmp, i, value)

    if level == 2:
        for i in range(planes):
            one(i)
    else:
        loop(0, planes, one, 2)


def field_plane(b, fine_row, count):
    return lambda x: b[x, pl.ds(fine_row, 2 * count)]


def residual_plane(level, u, f, cx, cxm, cy, cz, diag, fine_row, count):
    span = pl.ds(0, ROWS[level])

    def left(x):
        here, total = spread(level, x, u, cx, cxm, cy, cz, span)
        return (f[x] + total - diag[x] * here)[fine_row : fine_row + 2 * count]

    return left


def add_coarse(level, u, coarse, tmp, first, last, fine_x, coarse_row, fine_row, count, keep=None):
    def one(i):
        trip = i - first
        value = coarse[i, pl.ds(coarse_row, count)]
        tmp[trip, pl.ds(0, count, stride=2)] = value
        tmp[trip, pl.ds(1, count, stride=2)] = value
        span = pl.ds(fine_row, 2 * count)
        for m, part in enumerate(refine(level, tmp[trip, pl.ds(0, 2 * count)])):
            x = fine_x + 4 * trip + m
            if keep is None or x in keep:
                u[x, span] = u[x, span] + part

    if level == 2:
        for i in range(first, last):
            one(i)
    else:
        loop(first, last, one, 2)


def side(offset, length, width, at):
    if offset == 0:
        return pl.ds(0, length), pl.ds(at, length)
    if offset == 1:
        return pl.ds(length - width, width), pl.ds(at - width, width)
    return pl.ds(0, width), pl.ds(at + length, width)


def kernel(nx, ny, f_in, b_in, out, *refs):
    fields = [refs[10 * level : 10 * level + 10] for level in range(4)]
    tmp, load_sem, send_sem, recv_sem = refs[40:]
    (b0, f0, u0, v0, cx0, cm0, cy0, cz0, d0, g0) = fields[0]
    (b1, f1, u1, v1, cx1, cm1, cy1, cz1, d1, g1) = fields[1]
    (b2, f2, u2, v2, cx2, cm2, cy2, cz2, d2, g2) = fields[2]
    (b3, f3, u3, v3, cx3, cm3, cy3, cz3, d3, g3) = fields[3]
    c0, c1, c2, c3 = [(level[4], level[5], level[6], level[7]) for level in fields]
    mx, my = lax.axis_index("gx"), lax.axis_index("gy")
    far = [(dx, dy) for dx in far_offsets(nx) for dy in (-2, -1, 0, 1, 2) if (dx, dy) != (0, 0)]

    def peer(dx, dy):
        return (lax.rem(mx + dx + nx, nx), lax.rem(my + dy + ny, ny))

    barrier = pltpu.get_barrier_semaphore()
    for dx, dy in NEAR:
        pl.semaphore_signal(barrier, inc=1, device_id=peer(dx, dy), device_id_type=MESH)

    inside = (pl.ds(5, OWN), pl.ds(8, OWN))
    load_b = pltpu.make_async_copy(b_in, b0.at[inside], load_sem.at[0])
    load_f = pltpu.make_async_copy(f_in, f0.at[inside], load_sem.at[1])
    load_b.start()
    load_f.start()
    pl.semaphore_wait(barrier, len(NEAR))

    started = []

    def send(source, target, dx, dy):
        number = len(started)
        copy = pltpu.make_async_remote_copy(
            src_ref=source,
            dst_ref=target,
            send_sem=send_sem.at[number],
            recv_sem=recv_sem.at[number],
            device_id=peer(dx, dy),
            device_id_type=MESH,
        )
        copy.start()
        started.append(copy)
        return copy

    def send_0(dx, dy, wide, skip=0):
        copies = []
        for source, target, width in ((b_in, b0, wide), (f_in, f0, wide - 1)):
            from_x, to_x = side(dx, OWN, width, 5)
            if skip:
                count = 1
                if dx == 1:
                    from_x, to_x = pl.ds(from_x.start, count), pl.ds(to_x.start, count)
                else:
                    from_x = pl.ds(width - 1, count)
                    to_x = pl.ds(5 + OWN + width - 1, count)
            from_y, to_y = side(dy, OWN, width, 8)
            copies.append(send(source.at[from_x, from_y], target.at[to_x, to_y], dx, dy))
        return copies

    def arrive(copies):
        for copy in copies:
            copy.wait_recv()

    along_y = send_0(0, 1, 5) + send_0(0, -1, 5)
    along_x = send_0(1, 0, 4) + send_0(-1, 0, 4)
    for dx in (1, -1):
        for dy in (1, -1):
            along_x += send_0(dx, dy, 4)

    def send_1(field):
        copies = []
        for dx, dy in NEAR:
            from_x, to_x = side(dx, 8, 3, 4)
            from_y, to_y = side(dy, 16, 8, 8)
            from_x = pl.ds(from_x.start + 4, from_x.size)
            from_y = pl.ds(from_y.start + 8, from_y.size)
            copies.append(send(field.at[from_x, from_y], field.at[to_x, to_y], dx, dy))
        return copies

    def block_2(field, dx, dy):
        return field.at[pl.ds(5 + 2 * dx, 2), pl.ds(16 + 8 * dy, 8)]

    def send_2(field, corners):
        return [
            send(block_2(field, 0, 0), block_2(field, -dx, -dy), dx, dy)
            for dx, dy in far
            if corners or abs(dx) + abs(dy) < 4
        ]

    def finish_2(field, copies):
        for copy in copies:
            copy.wait_recv()
        if nx == 4:
            for p in (1, 2):
                field[p + 8] = field[p]

    load_b.wait()
    restrict(0, field_plane(b0, 8, 16), b1, tmp, 5, 8, 16, 4, 8)
    restrict(1, field_plane(b1, 8, 8), b2, tmp, 4, 2, 8, 5, 16)
    load_f.wait()
    arrive(along_y)
    build(0, 6, 36, b0, *c0, d0, g0, f0, u0)
    sweep(0, 7, 35, u0, v0, f0, *c0, g0)
    arrive(along_x)
    middle_b = send_1(b1)
    outer = []
    for dx in (1, -1):
        outer += send_0(dx, 0, 5, 1)
    coarse_b = send_2(b2, True)
    build(0, 2, 6, b0, *c0, d0, g0, f0, u0)
    build(0, 36, 40, b0, *c0, d0, g0, f0, u0)
    sweep(0, 3, 7, u0, v0, f0, *c0, g0)
    sweep(0, 35, 39, u0, v0, f0, *c0, g0)
    sweep(0, 4, 38, v0, u0, f0, *c0, g0)
    restrict(0, residual_plane(0, u0, f0, *c0, d0, 8, 16), f1, tmp, 5, 8, 16, 4, 8)
    middle_f = send_1(f1)
    arrive(middle_b)
    build(1, 1, 15, b1, *c1, d1, g1)
    arrive(outer)
    build(0, 1, 2, b0, *c0, d0, g0, f0, u0)
    build(0, 40, 41, b0, *c0, d0, g0, f0, u0)
    for x in (2, 39):
        sweep(0, x, x + 1, u0, v0, f0, *c0, g0)
    for x in (3, 38):
        sweep(0, x, x + 1, v0, u0, f0, *c0, g0)
    arrive(middle_f)

    first_sweep(1, 1, 15, u1, f1, g1)
    sweep(1, 1, 15, u1, v1, f1, *c1, g1)
    sweep(1, 1, 15, v1, u1, f1, *c1, g1)
    restrict(1, residual_plane(1, u1, f1, *c1, d1, 8, 8), f2, tmp, 4, 2, 8, 5, 16)
    coarse_f = send_2(f2, False)
    finish_2(b2, coarse_b)
    restrict(2, field_plane(b2, 0, 20), b3, tmp, 1, 3, 20, 1, 0, 10)
    build(2, 1, 11, b2, *c2, d2, g2)
    build(3, 1, 4, b3, *c3, d3, g3)
    finish_2(f2, coarse_f)

    first_sweep(2, 1, 11, u2, f2, g2)
    sweep(2, 1, 11, u2, v2, f2, *c2, g2)
    sweep(2, 1, 11, v2, u2, f2, *c2, g2)
    restrict(2, residual_plane(2, u2, f2, *c2, d2, 0, 20), f3, tmp, 1, 3, 20, 1, 0, 10)

    first_sweep(3, 1, 4, u3, f3, g3)
    sweep(3, 1, 4, u3, v3, f3, *c3, g3)
    sweep(3, 1, 4, v3, u3, f3, *c3, g3)
    sweep(3, 1, 4, u3, v3, f3, *c3, g3)
    sweep(3, 1, 4, v3, u3, f3, *c3, g3)

    add_coarse(2, u2, u3, tmp, 1, 3, 1, 4, 8, 12, (4, 5, 6, 7))
    middle = pl.ds(8, 24)
    sweep(2, 4, 8, u2, v2, f2, *c2, g2, middle)
    sweep(2, 4, 8, v2, u2, f2, *c2, g2, middle)

    add_coarse(1, u1, u2, tmp, 4, 8, 0, 12, 0, 16)
    sweep(1, 2, 14, u1, v1, f1, *c1, g1)
    sweep(1, 3, 13, v1, u1, f1, *c1, g1)

    add_coarse(0, u0, u1, tmp, 3, 13, 1, 4, 0, 24)
    sweep(0, 4, 38, u0, v0, f0, *c0, g0)

    whole = pl.ds(0, ROWS[0])

    def last(x):
        here, total = spread(0, x, v0, *c0, whole)
        value = (1.0 - OMEGA) * here + g0[x] * (f0[x] + total)
        out[x - 5] = value[8:40]

    loop(5, 37, last, 4)
    for copy in started:
        copy.wait_send()


def solution(mesh):
    nx, ny = mesh.shape["gx"], mesh.shape["gy"]
    far = len(far_offsets(nx)) * 5 - 1
    copies = 20 + 2 * len(NEAR) + 2 * far
    shapes = []
    for planes, height in zip(PLANES, ROWS):
        shapes += [pltpu.VMEM((planes, height, 128), F32)] * 10

    def per_device(source, inverse_density):
        return pl.pallas_call(
            functools.partial(kernel, nx, ny),
            out_shape=jax.ShapeDtypeStruct(source.shape, F32),
            in_specs=[pl.BlockSpec(memory_space=pl.ANY)] * 2,
            out_specs=pl.BlockSpec(memory_space=pltpu.VMEM),
            scratch_shapes=shapes
            + [
                pltpu.VMEM((20, 48, 128), F32),
                pltpu.SemaphoreType.DMA((2,)),
                pltpu.SemaphoreType.DMA((copies,)),
                pltpu.SemaphoreType.DMA((copies,)),
            ],
            compiler_params=pltpu.CompilerParams(collective_id=0, has_side_effects=True),
        )(source, inverse_density)

    placed = (P("gx", "gy", None), P("gx", "gy", None))
    return jax.shard_map(
        per_device, mesh=mesh, in_specs=placed, out_specs=P("gx", "gy", None), check_vma=False
    )
```

profile of v0, /device:TPU:0, one launch (start us, length us, event | category | flops | bytes accessed | tf_op | source)
XLA Modules:
  0.0 44.7 jit_solution(7259928731550819055)
XLA Ops:
  0.0 42.9 %shard_map.28 = f32[32,32,128]{2,1,0:T(8,128)} custom-call(f32[32,32,128]{2,1,0:T(8,128)} %f_in.1, f32[32,32,128]{2,1,0:T(8,128)} %b_in.1), custom_call_target="tpu_custom_call" | custom-call | tf_op jit(solution)/shard_map/pallas_call | solution.py:441
  42.9 1.9 %copy.4 = f32[32,32,128]{2,1,0:T(8,128)} copy(f32[32,32,128]{2,1,0:T(8,128)} %shard_map.28) | data formatting | bytes 1048576
where the time goes:
time: 44.9 us; the launch traced here: 44.7 us
  Pallas kernels  42.9 us (96%)
  local copies, waits for them, and re-layouts  1.87 us (4%)
    pallas_call x1, Pallas kernels, per_device(): pl.pallas_call(functools.partial(kernel, nx, ny), out_shape=jax.ShapeDtyp...  42.9 us
    unnamed x1, local copies, waits for them, and re-layouts  1.87 us

commit v1 on v0

v1 whole, which is shorter than its diff:
```python
import functools

import jax
import jax.numpy as jnp
from jax import lax
from jax.experimental import pallas as pl
from jax.experimental.pallas import tpu as pltpu
from jax.sharding import PartitionSpec as P

MESH = pl.DeviceIdType.MESH
OMEGA = 0.8
F32 = jnp.float32

PLANES = (42, 16, 12, 5)
ROWS = (48, 40, 48, 32)
AT = (5, 6, 16, 8)
SPAN = ((1, 40), (2, 24), (1, 40), (2, 16))
BUILD = ((1, 40), (1, 32), (1, 40), (2, 16))
OWN = 32
NEAR = [(dx, dy) for dx in (1, -1, 0) for dy in (0, 1, -1) if (dx, dy) != (0, 0)]


def far_offsets(peers):
    return (-1, 0, 1, 2) if peers == 4 else (-2, -1, 0, 1, 2)


def lanes(value, shift):
    return pltpu.roll(value, shift % 128, 1)


def rows(value, shift):
    return pltpu.roll(value, shift % value.shape[0], 0)


def lane_index(height):
    return lax.broadcasted_iota(jnp.int32, (height, 128), 1)


def swap_lanes(value, step):
    low = (lane_index(value.shape[0]) & step) == 0
    return jnp.where(low, lanes(value, -step), lanes(value, step))


def loop(first, last, body, unroll=2):
    count = last - first
    whole = count // unroll if count > unroll else 0

    def step(trip, carry):
        for inner in range(unroll):
            body(first + trip * unroll + inner)
        return carry

    if whole:
        lax.fori_loop(0, whole, step, 0)
    for index in range(first + whole * unroll, last):
        body(index)


def bit(number, height):
    return (lane_index(height) & number) != 0


def place_in_group(level, height):
    return lane_index(height) & (2**level - 1)


def next_x(level, here, after):
    if level == 0:
        return after
    size = 2**level
    last = place_in_group(level, here.shape[0]) == size - 1
    return jnp.where(last, lanes(after, size - 1), lanes(here, -1))


def previous_x(level, here, before):
    if level == 0:
        return before
    size = 2**level
    first = place_in_group(level, here.shape[0]) == 0
    return jnp.where(first, lanes(before, 1 - size), lanes(here, 1))


def pair(level, left, right):
    return (2.0 * 0.25**level) * left * right / (left + right)


def build(level, planes, wrap, b, cx, cxm, cy, cz, czm, diag, gain, f=None, u=None):
    at, height = BUILD[level]
    span, below, above = pl.ds(at, height), pl.ds(at - 1, height), pl.ds(at - 1, height + 8)
    step = 2**level
    lane = lane_index(height)
    top = lane >= 128 - step
    ends = top | (lane < step)

    def along_y(x):
        cy[x, above] = pair(level, b[x, above], b[x, pl.ds(at, height + 8)])

    def one(x, carry):
        c_before, here = carry
        after = b[wrap(x + 1), span]
        c_x = pair(level, here, next_x(level, here, after))
        c_m = previous_x(level, c_x, c_before)
        c_z = jnp.where(top, 0.0, pair(level, here, lanes(here, -step)))
        c_zm = lanes(c_z, step)
        total = c_m + c_x + cy[x, span] + cy[x, below] + c_z + c_zm
        total = total + jnp.where(ends, (0.25**level) * here, 0.0)
        scaled = OMEGA / total
        cx[x, span] = c_x
        if level > 0:
            cxm[x, span] = c_m
            czm[x, span] = c_zm
        cz[x, span] = c_z
        diag[x, span] = total
        gain[x, span] = scaled
        if f is not None:
            u[x, span] = scaled * f[x, span]
        if not (isinstance(x, int) and x == planes[-1]):
            along_y(wrap(x + 1))
        return (c_x, after)

    first = planes[0]
    previous = wrap(first - 1)
    start = b[previous, span]
    before = pair(level, start, next_x(level, start, b[first, span]))
    if level == 0:
        cx[previous, span] = before
    along_y(first)
    carry = (before, b[first, span])
    if len(planes) < 16:
        for x in planes:
            carry = one(x, carry)
        return

    def two(trip, carry):
        carry = one(first + 2 * trip, carry)
        return one(first + 1 + 2 * trip, carry)

    lax.fori_loop(0, len(planes) // 2, two, carry)


def first_sweep(level, planes, u, f, gain):
    span = pl.ds(*BUILD[level])
    for x in planes:
        u[x, span] = gain[x, span] * f[x, span]


def gather(x, u, cx, cxm, cy, cz, czm, at, height):
    span, below = pl.ds(at, height), pl.ds(at - 1, height)
    here = u[x, span]
    along_z = cz[x, span]
    total = cx[x, span] * u[x + 1, span] + cx[x - 1, span] * u[x - 1, span]
    total = total + (cy[x, span] * u[x, pl.ds(at + 1, height)] + cy[x, below] * u[x, below])
    total = total + (along_z * lanes(here, -1) + lanes(along_z * here, 1))
    return here, total


def sweep(first, last, source, target, f, coefs, gain, unroll=4):
    at, height = SPAN[0]
    span = pl.ds(at, height)

    def one(x):
        here, total = gather(x, source, *coefs, at, height)
        target[x, span] = (1.0 - OMEGA) * here + gain[x, span] * (f[x, span] + total)

    loop(first, last, one, unroll)


def packed(level, wrap, u, cx, cxm, cy, cz, czm, at, height):
    span, below = pl.ds(at, height), pl.ds(at - 1, height)
    step = 2**level
    place = place_in_group(level, height)
    is_first, is_last = place == 0, place == step - 1
    kept = {}

    def shifted(x, by):
        if (x, by) not in kept:
            kept[x, by] = lanes(u[x, span], by)
        return kept[x, by]

    def at_plane(x):
        here = u[x, span]
        upper, lower = shifted(x, -step), shifted(x, step)
        after = lanes(jnp.where(is_first, shifted(wrap(x + 1), step), here), -1)
        before = lanes(jnp.where(is_last, shifted(wrap(x - 1), -step), here), 1)
        total = cx[x, span] * after + cxm[x, span] * before
        total = total + (cy[x, span] * u[x, pl.ds(at + 1, height)] + cy[x, below] * u[x, below])
        total = total + (cz[x, span] * upper + czm[x, span] * lower)
        return here, total

    return at_plane


def sweep_packed(level, planes, wrap, source, target, f, coefs, gain, rows_at=None):
    at, height = SPAN[level] if rows_at is None else rows_at
    span = pl.ds(at, height)
    at_plane = packed(level, wrap, source, *coefs, at, height)
    for x in planes:
        here, total = at_plane(x)
        target[x, span] = (1.0 - OMEGA) * here + gain[x, span] * (f[x, span] + total)


def coarsen(level, values):
    height = values[0].shape[0]
    if level == 0:
        even = ~bit(1, height)
        left, right = values[0] + values[1], values[2] + values[3]
        return jnp.where(even, left, right) + jnp.where(even, lanes(left, -1), lanes(right, 1))
    size = 2**level
    sums = []
    for value in values:
        value = value + swap_lanes(value, 1)
        value = value + swap_lanes(value, size)
        if level == 2:
            value = jnp.where(bit(2, height) == bit(1, height), value, swap_lanes(value, 2))
        sums.append(value)
    low, high = (1, 2) if level == 1 else (2, 4)
    lower = jnp.where(bit(low, height), sums[1], sums[0])
    upper = jnp.where(bit(low, height), sums[3], sums[2])
    return jnp.where(bit(high, height), upper, lower)


def refine(level, value):
    height = value.shape[0]
    if level == 0:
        other = swap_lanes(value, 1)
        low = jnp.where(bit(1, height), other, value)
        high = jnp.where(bit(1, height), value, other)
        return [low, low, high, high]
    outer, inner = (2, 1) if level == 1 else (4, 2)
    other = swap_lanes(value, outer)
    result = []
    for half in (jnp.where(bit(outer, height), other, value), jnp.where(bit(outer, height), value, other)):
        swapped = swap_lanes(half, inner)
        result.append(jnp.where(bit(inner, height), swapped, half))
        result.append(jnp.where(bit(inner, height), half, swapped))
    if level == 2:
        same = bit(2, height) == bit(1, height)
        result = [jnp.where(same, part, swap_lanes(part, 1)) for part in result]
    return result


def pair_rows(tmp, slot, value):
    count = value.shape[0] // 2
    tmp[slot, pl.ds(0, 2 * count)] = value
    return tmp[slot, pl.ds(0, count, stride=2)] + tmp[slot, pl.ds(1, count, stride=2)]


def double_rows(tmp, slot, value):
    count = value.shape[0]
    tmp[slot, pl.ds(0, count, stride=2)] = value
    tmp[slot, pl.ds(1, count, stride=2)] = value
    return tmp[slot, pl.ds(0, 2 * count)]


def restrict(level, plane, target, tmp, fine_x, planes, count, at_x, at_row, limit=None):
    def one(i):
        parts = [fine_x + 4 * i + m for m in range(4)]
        if level == 0:
            summed = pair_rows(tmp, i, coarsen(level, [plane(part) for part in parts]))
        else:
            values = []
            for m, part in enumerate(parts):
                part = part if limit is None else min(part, limit)
                values.append(pair_rows(tmp, (4 * i + m) % 20, plane(part)))
            summed = coarsen(level, values)
        target[at_x + i, pl.ds(at_row, count)] = 0.125 * summed

    if level == 0:
        loop(0, planes, one, 2)
    else:
        for i in range(planes):
            one(i)


def field_plane(b, fine_row, count):
    return lambda x: b[x, pl.ds(fine_row, 2 * count)]


def residual_plane(u, f, coefs, diag, fine_row, count):
    def left(x):
        here, total = gather(x, u, *coefs, fine_row, 2 * count)
        span = pl.ds(fine_row, 2 * count)
        return f[x, span] + total - diag[x, span] * here

    return left


def residual_packed(level, wrap, u, f, coefs, diag, fine_row, count):
    at_plane = packed(level, wrap, u, *coefs, fine_row, 2 * count)
    span = pl.ds(fine_row, 2 * count)

    def left(x):
        here, total = at_plane(x)
        return f[x, span] + total - diag[x, span] * here

    return left


def add_coarse(level, u, coarse, tmp, first, last, fine_x, coarse_row, fine_row, count, keep=None):
    span = pl.ds(fine_row, 2 * count)

    def one(i):
        trip = i - first
        parts = refine(level, coarse[i, pl.ds(coarse_row, count)])
        if level == 0:
            low, high = double_rows(tmp, 2 * trip, parts[0]), double_rows(tmp, 2 * trip + 1, parts[2])
            parts = [low, low, high, high]
        for m, part in enumerate(parts):
            x = fine_x + 4 * trip + m
            if keep is None or x in keep:
                if level > 0:
                    part = double_rows(tmp, (4 * trip + m) % 20, part)
                u[x, span] = u[x, span] + part

    if level == 0:
        loop(first, last, one, 2)
    else:
        for i in range(first, last):
            one(i)


def side(offset, length, width, at):
    if offset == 0:
        return pl.ds(0, length), pl.ds(at, length)
    if offset == 1:
        return pl.ds(length - width, width), pl.ds(at - width, width)
    return pl.ds(0, width), pl.ds(at + length, width)


def kernel(nx, ny, f_in, b_in, out, *refs):
    fields = [refs[11 * level : 11 * level + 11] for level in range(4)]
    tmp, load_sem, send_sem, recv_sem, send_2_sem, recv_2_sem, bulk = refs[44:]
    (b0, f0, u0, v0), (b1, f1, u1, v1), (b2, f2, u2, v2), (b3, f3, u3, v3) = [level[:4] for level in fields]
    c0, c1, c2, c3 = [level[4:9] for level in fields]
    (d0, g0), (d1, g1), (d2, g2), (d3, g3) = [level[9:] for level in fields]
    y0, y1, y2, y3 = AT
    mx, my = lax.axis_index("gx"), lax.axis_index("gy")
    far = [(dx, dy) for dx in far_offsets(nx) for dy in (-2, -1, 0, 1, 2) if (dx, dy) != (0, 0)]

    def peer(dx, dy):
        return (lax.rem(mx + dx + nx, nx), lax.rem(my + dy + ny, ny))

    barrier = pltpu.get_barrier_semaphore()
    for dx, dy in NEAR:
        pl.semaphore_signal(barrier, inc=1, device_id=peer(dx, dy), device_id_type=MESH)

    inside = (pl.ds(5, OWN), pl.ds(y0, OWN))
    load_b = pltpu.make_async_copy(b_in, b0.at[inside], load_sem.at[0])
    load_f = pltpu.make_async_copy(f_in, f0.at[inside], load_sem.at[1])
    load_b.start()
    load_f.start()
    pl.semaphore_wait(barrier, len(NEAR))

    started = []

    def send(source, target, dx, dy):
        number = len(started)
        copy = pltpu.make_async_remote_copy(
            src_ref=source,
            dst_ref=target,
            send_sem=send_sem.at[number],
            recv_sem=recv_sem.at[number],
            device_id=peer(dx, dy),
            device_id_type=MESH,
        )
        copy.start()
        started.append(copy)
        return copy

    def send_0(dx, dy, wide, skip=0):
        copies = []
        for source, target, width in ((b_in, b0, wide), (f_in, f0, wide - 1)):
            from_x, to_x = side(dx, OWN, width, 5)
            if skip:
                count = 1
                if dx == 1:
                    from_x, to_x = pl.ds(from_x.start, count), pl.ds(to_x.start, count)
                else:
                    from_x = pl.ds(width - 1, count)
                    to_x = pl.ds(5 + OWN + width - 1, count)
            from_y, to_y = side(dy, OWN, width, y0)
            copies.append(send(source.at[from_x, from_y], target.at[to_x, to_y], dx, dy))
        return copies

    def arrive(copies):
        for copy in copies:
            copy.wait_recv()

    along_y = send_0(0, 1, 5) + send_0(0, -1, 5)
    along_x = send_0(1, 0, 4) + send_0(-1, 0, 4)
    for dx in (1, -1):
        for dy in (1, -1):
            along_x += send_0(dx, dy, 4)

    def send_1(field):
        copies = []
        for dx, dy in NEAR:
            from_x, to_x = side(dx, 8, 3, 4)
            from_y, to_y = side(dy, 16, 6, y1)
            from_x = pl.ds(from_x.start + 4, from_x.size)
            from_y = pl.ds(from_y.start + y1, from_y.size)
            copies.append(send(field.at[from_x, from_y], field.at[to_x, to_y], dx, dy))
        return copies

    def block_2(field, dx, dy):
        return field.at[pl.ds(5 + 2 * dx, 2), pl.ds(y2 + 8 * dy, 8)]

    def send_2(field, number, corners):
        count = 0
        for dx, dy in far:
            if corners or abs(dx) + abs(dy) < 4:
                pltpu.make_async_remote_copy(
                    src_ref=block_2(field, 0, 0),
                    dst_ref=block_2(field, -dx, -dy),
                    send_sem=send_2_sem.at[number],
                    recv_sem=recv_2_sem.at[number],
                    device_id=peer(dx, dy),
                    device_id_type=MESH,
                ).start()
                count += 1
        return bulk.at[pl.ds(0, 2 * count)]

    def wait_2(whole, sems, number):
        pltpu.make_async_copy(whole, whole, sems.at[number]).wait()

    def sent(copies):
        for copy in copies:
            copy.wait_send()

    same = lambda x: x
    ring = nx == 4
    wrap_2 = (lambda x: (x - 1) % 8 + 1) if ring else same
    wrap_3 = (lambda x: (x - 1) % 2 + 1) if ring else same
    planes_1 = range(1, 15)
    inner_1 = range(2, 14)
    planes_2 = range(1, 9) if ring else range(1, 11)
    planes_3 = range(1, 3) if ring else range(1, 4)
    limit = 8 if ring else 10

    load_b.wait()
    restrict(0, field_plane(b0, y0, 16), b1, tmp, 5, 8, 16, 4, y1)
    restrict(1, field_plane(b1, y1, 8), b2, tmp, 4, 2, 8, 5, y2)
    load_f.wait()
    arrive(along_y)
    build(0, range(6, 36), same, b0, *c0, d0, g0, f0, u0)
    sweep(7, 35, u0, v0, f0, c0, g0)
    arrive(along_x)
    middle_b = send_1(b1)
    outer = []
    for dx in (1, -1):
        outer += send_0(dx, 0, 5, 1)
    whole_b = send_2(b2, 0, True)
    build(0, range(2, 6), same, b0, *c0, d0, g0, f0, u0)
    build(0, range(36, 40), same, b0, *c0, d0, g0, f0, u0)
    sweep(3, 7, u0, v0, f0, c0, g0)
    sweep(35, 39, u0, v0, f0, c0, g0)
    sweep(4, 38, v0, u0, f0, c0, g0)
    restrict(0, residual_plane(u0, f0, c0, d0, y0, 16), f1, tmp, 5, 8, 16, 4, y1)
    middle_f = send_1(f1)
    arrive(middle_b)
    build(1, planes_1, same, b1, *c1, d1, g1)
    arrive(outer)
    build(0, range(1, 2), same, b0, *c0, d0, g0, f0, u0)
    build(0, range(40, 41), same, b0, *c0, d0, g0, f0, u0)
    for x in (2, 39):
        sweep(x, x + 1, u0, v0, f0, c0, g0)
    for x in (3, 38):
        sweep(x, x + 1, v0, u0, f0, c0, g0)
    sent(along_y + along_x + middle_b + outer)
    arrive(middle_f)

    first_sweep(1, planes_1, u1, f1, g1)
    sweep_packed(1, inner_1, same, u1, v1, f1, c1, g1)
    sweep_packed(1, inner_1, same, v1, u1, f1, c1, g1)
    restrict(1, residual_packed(1, same, u1, f1, c1, d1, y1, 8), f2, tmp, 4, 2, 8, 5, y2)
    whole_f = send_2(f2, 1, False)
    wait_2(whole_b, recv_2_sem, 0)
    restrict(2, field_plane(b2, 0, 20), b3, tmp, 1, len(planes_3), 20, 1, 0, limit)
    build(2, planes_2, wrap_2, b2, *c2, d2, g2)
    build(3, planes_3, wrap_3, b3, *c3, d3, g3)
    sent(middle_f)
    wait_2(whole_b, send_2_sem, 0)
    wait_2(whole_f, recv_2_sem, 1)

    first_sweep(2, planes_2, u2, f2, g2)
    sweep_packed(2, planes_2, wrap_2, u2, v2, f2, c2, g2)
    sweep_packed(2, planes_2, wrap_2, v2, u2, f2, c2, g2)
    restrict(
        2, residual_packed(2, wrap_2, u2, f2, c2, d2, 4, 16), f3, tmp, 1, len(planes_3), 16, 1, 2, limit
    )

    first_sweep(3, planes_3, u3, f3, g3)
    for _ in range(2):
        sweep_packed(3, planes_3, wrap_3, u3, v3, f3, c3, g3)
        sweep_packed(3, planes_3, wrap_3, v3, u3, f3, c3, g3)

    add_coarse(2, u2, u3, tmp, 1, 3, 1, y3 - 2, y2 - 4, 8, (4, 5, 6, 7))
    middle = (y2 - 4, 16)
    sweep_packed(2, range(4, 8), same, u2, v2, f2, c2, g2, middle)
    sweep_packed(2, range(4, 8), same, v2, u2, f2, c2, g2, middle)

    add_coarse(1, u1, u2, tmp, 4, 8, 0, y2 - 2, y1 - 4, 12, inner_1)
    sweep_packed(1, range(3, 13), same, u1, v1, f1, c1, g1)
    sweep_packed(1, range(3, 13), same, v1, u1, f1, c1, g1)

    add_coarse(0, u0, u1, tmp, 3, 13, 1, y1 - 2, 1, 20)
    sweep(4, 38, u0, v0, f0, c0, g0)

    own = pl.ds(y0, OWN)

    def last(x):
        here, total = gather(x, v0, *c0, y0, OWN)
        out[x - 5] = (1.0 - OMEGA) * here + g0[x, own] * (f0[x, own] + total)

    loop(5, 37, last, 4)
    wait_2(whole_f, send_2_sem, 1)


def solution(mesh):
    nx, ny = mesh.shape["gx"], mesh.shape["gy"]
    copies = 20 + 2 * len(NEAR)
    shapes = []
    for planes, height in zip(PLANES, ROWS):
        shapes += [pltpu.VMEM((planes, height + 8, 128), F32)] + [pltpu.VMEM((planes, height, 128), F32)] * 10

    def per_device(source, inverse_density):
        return pl.pallas_call(
            functools.partial(kernel, nx, ny),
            out_shape=jax.ShapeDtypeStruct(source.shape, F32),
            in_specs=[pl.BlockSpec(memory_space=pl.ANY)] * 2,
            out_specs=pl.BlockSpec(memory_space=pltpu.VMEM),
            scratch_shapes=shapes
            + [
                pltpu.VMEM((20, 48, 128), F32),
                pltpu.SemaphoreType.DMA((2,)),
                pltpu.SemaphoreType.DMA((copies,)),
                pltpu.SemaphoreType.DMA((copies,)),
                pltpu.SemaphoreType.DMA((2,)),
                pltpu.SemaphoreType.DMA((2,)),
                pltpu.VMEM((48, 8, 128), F32),
            ],
            compiler_params=pltpu.CompilerParams(collective_id=0, has_side_effects=True),
        )(source, inverse_density)

    placed = (P("gx", "gy", None), P("gx", "gy", None))
    return jax.shard_map(
        per_device, mesh=mesh, in_specs=placed, out_specs=P("gx", "gy", None), check_vma=False
    )
```

time: 44.9 us -> 40.8 us (0.909)
  Pallas kernels: 42.9 us -> 38.7 us
    pallas_call x1, Pallas kernels: 42.9 us -> 38.7 us  [per_device(): pl.pallas_call(functools.partial(kernel, nx, ny), out_shape=jax.ShapeDtyp...]
where the time goes in v1:
time: 40.8 us; the launch traced here: 40.6 us
  Pallas kernels  38.7 us (95%)
  local copies, waits for them, and re-layouts  1.87 us (5%)
    pallas_call x1, Pallas kernels, per_device(): pl.pallas_call(functools.partial(kernel, nx, ny), out_shape=jax.ShapeDtyp...  38.7 us
    unnamed x1, local copies, waits for them, and re-layouts  1.87 us

profile of v1, /device:TPU:0, one launch (start us, length us, event | category | flops | bytes accessed | tf_op | source)
XLA Modules:
  0.0 40.6 jit_solution(9888015842779697305)
XLA Ops:
  0.0 38.7 %shard_map.28 = f32[32,32,128]{2,1,0:T(8,128)} custom-call(f32[32,32,128]{2,1,0:T(8,128)} %f_in.1, f32[32,32,128]{2,1,0:T(8,128)} %b_in.1), custom_call_target="tpu_custom_call" | custom-call | tf_op jit(solution)/shard_map/pallas_call | solution.py:527
  38.7 1.9 %copy.4 = f32[32,32,128]{2,1,0:T(8,128)} copy(f32[32,32,128]{2,1,0:T(8,128)} %shard_map.28) | data formatting | bytes 1048576

commit v2 on v1

--- a/solution.py
+++ b/solution.py
@@ -1,4 +1,5 @@
 import functools
+import math
 
 import jax
 import jax.numpy as jnp
@@ -17,6 +18,7 @@
 SPAN = ((1, 40), (2, 24), (1, 40), (2, 16))
 BUILD = ((1, 40), (1, 32), (1, 40), (2, 16))
 OWN = 32
+X_0, Y_0, OUTER, B_1, F_1, B_2, F_2 = range(7)
 NEAR = [(dx, dy) for dx in (1, -1, 0) for dy in (0, 1, -1) if (dx, dy) != (0, 0)]
 
 
@@ -84,16 +86,18 @@
     return (2.0 * 0.25**level) * left * right / (left + right)
 
 
-def build(level, planes, wrap, b, cx, cxm, cy, cz, czm, diag, gain, f=None, u=None):
-    at, height = BUILD[level]
-    span, below, above = pl.ds(at, height), pl.ds(at - 1, height), pl.ds(at - 1, height + 8)
+def build(level, planes, wrap, b, cx, cxm, cy, cz, czm, diag, gain, f=None, u=None, rows=None, faces=None):
+    at, height = BUILD[level] if rows is None else rows
+    span, below = pl.ds(at, height), pl.ds(at - 1, height)
+    low, faces = (at - 1, height + 8) if faces is None else faces
     step = 2**level
     lane = lane_index(height)
     top = lane >= 128 - step
     ends = top | (lane < step)
 
     def along_y(x):
-        cy[x, above] = pair(level, b[x, above], b[x, pl.ds(at, height + 8)])
+        lower = pl.ds(low, faces)
+        cy[x, lower] = pair(level, b[x, lower], b[x, pl.ds(low + 1, faces)])
 
     def one(x, carry):
         c_before, here = carry
@@ -131,11 +135,14 @@
             carry = one(x, carry)
         return
 
-    def two(trip, carry):
-        carry = one(first + 2 * trip, carry)
-        return one(first + 1 + 2 * trip, carry)
-
-    lax.fori_loop(0, len(planes) // 2, two, carry)
+    group = 5 if height > 8 else 15
+
+    def some(trip, carry):
+        for inner in range(group):
+            carry = one(first + group * trip + inner, carry)
+        return carry
+
+    lax.fori_loop(0, len(planes) // group, some, carry)
 
 
 def first_sweep(level, planes, u, f, gain):
@@ -154,8 +161,9 @@
     return here, total
 
 
-def sweep(first, last, source, target, f, coefs, gain, unroll=4):
-    at, height = SPAN[0]
+def sweep(first, last, source, target, f, coefs, gain, rows=SPAN[0], unroll=None):
+    at, height = rows
+    unroll = (84 if height > 8 else 112) // (-(-height // 8)) if unroll is None else unroll
     span = pl.ds(at, height)
 
     def one(x):
@@ -329,10 +337,11 @@
 
 def kernel(nx, ny, f_in, b_in, out, *refs):
     fields = [refs[11 * level : 11 * level + 11] for level in range(4)]
-    tmp, load_sem, send_sem, recv_sem, send_2_sem, recv_2_sem, bulk = refs[44:]
+    tmp, load_sem, send_sem, recv_sem, bulk = refs[44:]
     (b0, f0, u0, v0), (b1, f1, u1, v1), (b2, f2, u2, v2), (b3, f3, u3, v3) = [level[:4] for level in fields]
     c0, c1, c2, c3 = [level[4:9] for level in fields]
     (d0, g0), (d1, g1), (d2, g2), (d3, g3) = [level[9:] for level in fields]
+    w0 = c0[4]
     y0, y1, y2, y3 = AT
     mx, my = lax.axis_index("gx"), lax.axis_index("gy")
     far = [(dx, dy) for dx in far_offsets(nx) for dy in (-2, -1, 0, 1, 2) if (dx, dy) != (0, 0)]
@@ -349,26 +358,36 @@
     load_f = pltpu.make_async_copy(f_in, f0.at[inside], load_sem.at[1])
     load_b.start()
     load_f.start()
+    load_b.wait()
+    restrict(0, field_plane(b0, y0, 16), b1, tmp, 5, 8, 16, 4, y1)
+    restrict(1, field_plane(b1, y1, 8), b2, tmp, 4, 2, 8, 5, y2)
+    load_f.wait()
+    same = lambda x: x
+    build(0, range(6, 36), same, b0, *c0, d0, g0, f0, u0, (y0 + 1, OWN - 2), (y0, OWN - 1))
     pl.semaphore_wait(barrier, len(NEAR))
 
-    started = []
-
-    def send(source, target, dx, dy):
-        number = len(started)
+    sizes = {}
+
+    def send(source, target, dx, dy, group):
         copy = pltpu.make_async_remote_copy(
             src_ref=source,
             dst_ref=target,
-            send_sem=send_sem.at[number],
-            recv_sem=recv_sem.at[number],
+            send_sem=send_sem.at[0],
+            recv_sem=recv_sem.at[group],
             device_id=peer(dx, dy),
             device_id_type=MESH,
         )
         copy.start()
-        started.append(copy)
-        return copy
-
-    def send_0(dx, dy, wide, skip=0):
-        copies = []
+        sizes[group] = sizes.get(group, 0) + math.prod(source.shape[:-1])
+
+    def settle(sems, number, count):
+        whole = bulk.at[pl.ds(0, count)]
+        pltpu.make_async_copy(whole, whole, sems.at[number]).wait()
+
+    def arrive(group):
+        settle(recv_sem, group, sizes[group])
+
+    def send_0(dx, dy, wide, group, skip=0):
         for source, target, width in ((b_in, b0, wide), (f_in, f0, wide - 1)):
             from_x, to_x = side(dx, OWN, width, 5)
             if skip:
@@ -379,55 +398,24 @@
                     from_x = pl.ds(width - 1, count)
                     to_x = pl.ds(5 + OWN + width - 1, count)
             from_y, to_y = side(dy, OWN, width, y0)
-            copies.append(send(source.at[from_x, from_y], target.at[to_x, to_y], dx, dy))
-        return copies
-
-    def arrive(copies):
-        for copy in copies:
-            copy.wait_recv()
-
-    along_y = send_0(0, 1, 5) + send_0(0, -1, 5)
-    along_x = send_0(1, 0, 4) + send_0(-1, 0, 4)
-    for dx in (1, -1):
-        for dy in (1, -1):
-            along_x += send_0(dx, dy, 4)
-
-    def send_1(field):
-        copies = []
+            send(source.at[from_x, from_y], target.at[to_x, to_y], dx, dy, group)
+
+    def send_1(field, group):
         for dx, dy in NEAR:
             from_x, to_x = side(dx, 8, 3, 4)
             from_y, to_y = side(dy, 16, 6, y1)
             from_x = pl.ds(from_x.start + 4, from_x.size)
             from_y = pl.ds(from_y.start + y1, from_y.size)
-            copies.append(send(field.at[from_x, from_y], field.at[to_x, to_y], dx, dy))
-        return copies
+            send(field.at[from_x, from_y], field.at[to_x, to_y], dx, dy, group)
 
     def block_2(field, dx, dy):
         return field.at[pl.ds(5 + 2 * dx, 2), pl.ds(y2 + 8 * dy, 8)]
 
-    def send_2(field, number, corners):
-        count = 0
+    def send_2(field, group, corners):
         for dx, dy in far:
             if corners or abs(dx) + abs(dy) < 4:
-                pltpu.make_async_remote_copy(
-                    src_ref=block_2(field, 0, 0),
-                    dst_ref=block_2(field, -dx, -dy),
-                    send_sem=send_2_sem.at[number],
-                    recv_sem=recv_2_sem.at[number],
-                    device_id=peer(dx, dy),
-                    device_id_type=MESH,
-                ).start()
-                count += 1
-        return bulk.at[pl.ds(0, 2 * count)]
-
-    def wait_2(whole, sems, number):
-        pltpu.make_async_copy(whole, whole, sems.at[number]).wait()
-
-    def sent(copies):
-        for copy in copies:
-            copy.wait_send()
-
-    same = lambda x: x
+                send(block_2(field, 0, 0), block_2(field, -dx, -dy), dx, dy, group)
+
     ring = nx == 4
     wrap_2 = (lambda x: (x - 1) % 8 + 1) if ring else same
     wrap_3 = (lambda x: (x - 1) % 2 + 1) if ring else same
@@ -437,50 +425,64 @@
     planes_3 = range(1, 3) if ring else range(1, 4)
     limit = 8 if ring else 10
 
-    load_b.wait()
-    restrict(0, field_plane(b0, y0, 16), b1, tmp, 5, 8, 16, 4, y1)
-    restrict(1, field_plane(b1, y1, 8), b2, tmp, 4, 2, 8, 5, y2)
-    load_f.wait()
-    arrive(along_y)
-    build(0, range(6, 36), same, b0, *c0, d0, g0, f0, u0)
-    sweep(7, 35, u0, v0, f0, c0, g0)
-    arrive(along_x)
-    middle_b = send_1(b1)
-    outer = []
+    send_0(1, 0, 4, X_0)
+    send_0(-1, 0, 4, X_0)
+    send_0(0, 1, 5, Y_0)
+    send_0(0, -1, 5, Y_0)
     for dx in (1, -1):
-        outer += send_0(dx, 0, 5, 1)
-    whole_b = send_2(b2, 0, True)
+        for dy in (1, -1):
+            send_0(dx, dy, 4, X_0)
+
+    send_1(b1, B_1)
+    for dx in (1, -1):
+        send_0(dx, 0, 5, OUTER, 1)
+
+    def fold(first, count):
+        plane = residual_plane(w0, f0, c0, d0, y0, 16)
+        restrict(0, plane, f1, tmp, 5 + 4 * first, count, 16, 4 + first, y1)
+
+    sweep(7, 35, u0, v0, f0, c0, g0, (y0 + 2, OWN - 4))
+    sweep(8, 34, v0, w0, f0, c0, g0, (y0 + 3, OWN - 6))
+    arrive(Y_0)
+    for at in (1, 33):
+        build(0, range(6, 36), same, b0, *c0, d0, g0, f0, u0, (at, 8))
+    for at in (2, 32):
+        sweep(7, 35, u0, v0, f0, c0, g0, (at, 8))
+    for at in (3, 31):
+        sweep(8, 34, v0, w0, f0, c0, g0, (at, 8))
+    fold(1, 6)
+    arrive(X_0)
     build(0, range(2, 6), same, b0, *c0, d0, g0, f0, u0)
     build(0, range(36, 40), same, b0, *c0, d0, g0, f0, u0)
     sweep(3, 7, u0, v0, f0, c0, g0)
     sweep(35, 39, u0, v0, f0, c0, g0)
-    sweep(4, 38, v0, u0, f0, c0, g0)
-    restrict(0, residual_plane(u0, f0, c0, d0, y0, 16), f1, tmp, 5, 8, 16, 4, y1)
-    middle_f = send_1(f1)
-    arrive(middle_b)
+    sweep(4, 8, v0, w0, f0, c0, g0)
+    sweep(34, 38, v0, w0, f0, c0, g0)
+    fold(0, 1)
+    fold(7, 1)
+    send_1(f1, F_1)
+    send_2(b2, B_2, True)
+    arrive(B_1)
     build(1, planes_1, same, b1, *c1, d1, g1)
-    arrive(outer)
+    arrive(OUTER)
     build(0, range(1, 2), same, b0, *c0, d0, g0, f0, u0)
     build(0, range(40, 41), same, b0, *c0, d0, g0, f0, u0)
     for x in (2, 39):
         sweep(x, x + 1, u0, v0, f0, c0, g0)
     for x in (3, 38):
-        sweep(x, x + 1, v0, u0, f0, c0, g0)
-    sent(along_y + along_x + middle_b + outer)
-    arrive(middle_f)
+        sweep(x, x + 1, v0, w0, f0, c0, g0)
+    arrive(F_1)
 
     first_sweep(1, planes_1, u1, f1, g1)
     sweep_packed(1, inner_1, same, u1, v1, f1, c1, g1)
     sweep_packed(1, inner_1, same, v1, u1, f1, c1, g1)
     restrict(1, residual_packed(1, same, u1, f1, c1, d1, y1, 8), f2, tmp, 4, 2, 8, 5, y2)
-    whole_f = send_2(f2, 1, False)
-    wait_2(whole_b, recv_2_sem, 0)
+    send_2(f2, F_2, False)
+    arrive(B_2)
     restrict(2, field_plane(b2, 0, 20), b3, tmp, 1, len(planes_3), 20, 1, 0, limit)
     build(2, planes_2, wrap_2, b2, *c2, d2, g2)
     build(3, planes_3, wrap_3, b3, *c3, d3, g3)
-    sent(middle_f)
-    wait_2(whole_b, send_2_sem, 0)
-    wait_2(whole_f, recv_2_sem, 1)
+    arrive(F_2)
 
     first_sweep(2, planes_2, u2, f2, g2)
     sweep_packed(2, planes_2, wrap_2, u2, v2, f2, c2, g2)
@@ -503,8 +505,8 @@
     sweep_packed(1, range(3, 13), same, u1, v1, f1, c1, g1)
     sweep_packed(1, range(3, 13), same, v1, u1, f1, c1, g1)
 
-    add_coarse(0, u0, u1, tmp, 3, 13, 1, y1 - 2, 1, 20)
-    sweep(4, 38, u0, v0, f0, c0, g0)
+    add_coarse(0, w0, u1, tmp, 3, 13, 1, y1 - 2, 1, 20)
+    sweep(4, 38, w0, v0, f0, c0, g0)
 
     own = pl.ds(y0, OWN)
 
@@ -512,13 +514,12 @@
         here, total = gather(x, v0, *c0, y0, OWN)
         out[x - 5] = (1.0 - OMEGA) * here + g0[x, own] * (f0[x, own] + total)
 
-    loop(5, 37, last, 4)
-    wait_2(whole_f, send_2_sem, 1)
+    loop(5, 37, last, 16)
+    settle(send_sem, 0, sum(sizes.values()))
 
 
 def solution(mesh):
     nx, ny = mesh.shape["gx"], mesh.shape["gy"]
-    copies = 20 + 2 * len(NEAR)
     shapes = []
     for planes, height in zip(PLANES, ROWS):
         shapes += [pltpu.VMEM((planes, height + 8, 128), F32)] + [pltpu.VMEM((planes, height, 128), F32)] * 10
@@ -533,11 +534,9 @@
             + [
                 pltpu.VMEM((20, 48, 128), F32),
                 pltpu.SemaphoreType.DMA((2,)),
-                pltpu.SemaphoreType.DMA((copies,)),
-                pltpu.SemaphoreType.DMA((copies,)),
-                pltpu.SemaphoreType.DMA((2,)),
-                pltpu.SemaphoreType.DMA((2,)),
-                pltpu.VMEM((48, 8, 128), F32),
+                pltpu.SemaphoreType.DMA((1,)),
+                pltpu.SemaphoreType.DMA((7,)),
+                pltpu.VMEM((5120, 128), F32),
             ],
             compiler_params=pltpu.CompilerParams(collective_id=0, has_side_effects=True),
         )(source, inverse_density)

time: 40.8 us -> 35 us (0.86)
  Pallas kernels: 38.7 us -> 33 us
    pallas_call x1, Pallas kernels: 38.7 us -> 33 us  [per_device(): pl.pallas_call(functools.partial(kernel, nx, ny), out_shape=jax.ShapeDtyp...]
where the time goes in v2:
time: 35 us; the launch traced here: 34.8 us
  Pallas kernels  33 us (94%)
  local copies, waits for them, and re-layouts  1.87 us (5%)
    pallas_call x1, Pallas kernels, per_device(): pl.pallas_call(functools.partial(kernel, nx, ny), out_shape=jax.ShapeDtyp...  33 us
    unnamed x1, local copies, waits for them, and re-layouts  1.87 us

profile of v2, /device:TPU:0, one launch (start us, length us, event | category | flops | bytes accessed | tf_op | source)
XLA Modules:
  0.0 34.8 jit_solution(5454760634088642188)
XLA Ops:
  0.0 33.0 %shard_map.28 = f32[32,32,128]{2,1,0:T(8,128)} custom-call(f32[32,32,128]{2,1,0:T(8,128)} %f_in.1, f32[32,32,128]{2,1,0:T(8,128)} %b_in.1), custom_call_target="tpu_custom_call" | custom-call | tf_op jit(solution)/shard_map/pallas_call | solution.py:528
  33.0 1.9 %copy.4 = f32[32,32,128]{2,1,0:T(8,128)} copy(f32[32,32,128]{2,1,0:T(8,128)} %shard_map.28) | data formatting | bytes 1048576

commit v3 on v2

--- a/solution.py
+++ b/solution.py
@@ -188,8 +188,12 @@
     def at_plane(x):
         here = u[x, span]
         upper, lower = shifted(x, -step), shifted(x, step)
-        after = lanes(jnp.where(is_first, shifted(wrap(x + 1), step), here), -1)
-        before = lanes(jnp.where(is_last, shifted(wrap(x - 1), -step), here), 1)
+        if level == 3:
+            after = next_x(level, here, u[wrap(x + 1), span])
+            before = previous_x(level, here, u[wrap(x - 1), span])
+        else:
+            after = lanes(jnp.where(is_first, shifted(wrap(x + 1), step), here), -1)
+            before = lanes(jnp.where(is_last, shifted(wrap(x - 1), -step), here), 1)
         total = cx[x, span] * after + cxm[x, span] * before
         total = total + (cy[x, span] * u[x, pl.ds(at + 1, height)] + cy[x, below] * u[x, below])
         total = total + (cz[x, span] * upper + czm[x, span] * lower)
@@ -433,16 +437,16 @@
         for dy in (1, -1):
             send_0(dx, dy, 4, X_0)
 
+
+    def fold(first, count):
+        plane = residual_plane(w0, f0, c0, d0, y0, 16)
+        restrict(0, plane, f1, tmp, 5 + 4 * first, count, 16, 4 + first, y1)
+
+    sweep(7, 35, u0, v0, f0, c0, g0, (y0 + 2, OWN - 4))
+    sweep(8, 34, v0, w0, f0, c0, g0, (y0 + 3, OWN - 6))
     send_1(b1, B_1)
     for dx in (1, -1):
         send_0(dx, 0, 5, OUTER, 1)
-
-    def fold(first, count):
-        plane = residual_plane(w0, f0, c0, d0, y0, 16)
-        restrict(0, plane, f1, tmp, 5 + 4 * first, count, 16, 4 + first, y1)
-
-    sweep(7, 35, u0, v0, f0, c0, g0, (y0 + 2, OWN - 4))
-    sweep(8, 34, v0, w0, f0, c0, g0, (y0 + 3, OWN - 6))
     arrive(Y_0)
     for at in (1, 33):
         build(0, range(6, 36), same, b0, *c0, d0, g0, f0, u0, (at, 8))
@@ -538,7 +542,9 @@
                 pltpu.SemaphoreType.DMA((7,)),
                 pltpu.VMEM((5120, 128), F32),
             ],
-            compiler_params=pltpu.CompilerParams(collective_id=0, has_side_effects=True),
+            compiler_params=pltpu.CompilerParams(
+                collective_id=0, has_side_effects=True, vmem_limit_bytes=40 * 2**20
+            ),
         )(source, inverse_density)
 
     placed = (P("gx", "gy", None), P("gx", "gy", None))

time: 35 us -> 34.5 us (0.986)
  Pallas kernels: 33 us -> 31.4 us
  local copies, waits for them, and re-layouts: 1.87 us -> 2.88 us
    pallas_call x1, Pallas kernels: 33 us -> 31.4 us  [per_device(): pl.pallas_call(functools.partial(kernel, nx, ny), out_shape=jax.ShapeDtyp...]
    unnamed x1 -> x5, local copies, waits for them, and re-layouts: 1.87 us -> 2.88 us
where the time goes in v3:
time: 34.5 us; the launch traced here: 34.3 us
  Pallas kernels  31.4 us (91%)
  local copies, waits for them, and re-layouts  2.88 us (8%)
    pallas_call x1, Pallas kernels, per_device(): pl.pallas_call(functools.partial(kernel, nx, ny), out_shape=jax.ShapeDtyp...  31.4 us
    unnamed x5, local copies, waits for them, and re-layouts  2.88 us

profile of v3, /device:TPU:0, one launch (start us, length us, event | category | flops | bytes accessed | tf_op | source)
XLA Modules:
  0.0 34.3 jit_solution(7048288004547031651)
XLA Ops:
  0.0 0.0 copy-start
  0.0 1.0 %copy-done = f32[32,32,128]{2,1,0:T(8,128)S(1)} copy-done((f32[32,32,128]{2,1,0:T(8,128)S(1)}, f32[32,32,128]{2,1,0:T(8,128)}, u32[]{:S(2)}) %copy-start) | copy-done | bytes 524312
  1.0 0.0 copy-start.1
  1.0 1.0 %copy-done.1 = f32[32,32,128]{2,1,0:T(8,128)S(1)} copy-done((f32[32,32,128]{2,1,0:T(8,128)S(1)}, f32[32,32,128]{2,1,0:T(8,128)}, u32[]{:S(2)}) %copy-start.1) | copy-done | bytes 524312
  2.1 31.4 %shard_map.28 = f32[32,32,128]{2,1,0:T(8,128)S(1)} custom-call(f32[32,32,128]{2,1,0:T(8,128)S(1)} %copy-done, f32[32,32,128]{2,1,0:T(8,128)S(1)} %copy-done.1), custom_call_target="tpu_custom_call" | custom-call | tf_op jit(solution)/shard_map/pallas_call | solution.py:532
  33.5 0.8 %copy.4 = f32[32,32,128]{2,1,0:T(8,128)} copy(f32[32,32,128]{2,1,0:T(8,128)S(1)} %shard_map.28) | data formatting | bytes 1048576
Async XLA Ops:
  0.0 1.0 %copy-start = (f32[32,32,128]{2,1,0:T(8,128)S(1)}, f32[32,32,128]{2,1,0:T(8,128)}, u32[]{:S(2)}) copy-start(f32[32,32,128]{2,1,0:T(8,128)} %f_in.1) | copy-start | bytes 1572868
  1.0 1.0 %copy-start.1 = (f32[32,32,128]{2,1,0:T(8,128)S(1)}, f32[32,32,128]{2,1,0:T(8,128)}, u32[]{:S(2)}) copy-start(f32[32,32,128]{2,1,0:T(8,128)} %b_in.1) | copy-start | bytes 1572868
